TPU v7x, 512 devices: a whole 4x8x8 slice. The times are simulated.
512 devices in a mesh: expert: 16 (over y, core), dp: 32 (over z, x).
Axes of the slice: x: 4, y: 8, z: 8, core: 2. Of those that a mesh axis runs over, the one named last changes fastest.
Arguments:
- tokens: bfloat16 [768, 3072], P('dp'), may hold values from -6 to 6
- routes: int32 [768, 2], replicated, may hold values from 0 to 7, all different within a row; in each aligned block of 24 rows (0 to 23, 24 to 47, ...) at most 12 rows name the same one
- w_router: bfloat16 [3072, 8], replicated, may hold values from -0.109375 to 0.109375
- norm_gain: float32 [3072], replicated, may hold values from 0.25 to 1.75
- w_gate: bfloat16 [16, 3072, 4096], P('expert', None, 'dp'), may hold values from -0.109375 to 0.109375
- w_up: bfloat16 [16, 3072, 4096], P('expert', None, 'dp'), may hold values from -0.109375 to 0.109375
- w_down: bfloat16 [16, 4096, 3072], P('expert', 'dp'), may hold values from -0.09375 to 0.09375
- final_gain: float32 [3072], replicated, may hold values from 0.25 to 1.75
- head_weights: bfloat16 [4, 3072, 3072], P(None, 'dp', 'expert'), may hold values from -0.109375 to 0.109375
- vocab_proj: bfloat16 [3072, 16384], P('dp', 'expert'), may hold values from -0.21650635 to 0.21650635
Outputs:
- head_losses: float32 [4], replicated
- head_grads: float32 [4, 3072, 3072], P(None, 'dp', 'expert')
Inputs may be any that keep to these rules, and one draw needn't show every extreme that they name: `routes`: in each aligned block of 24 rows (one token block) no expert is named by more than 12 rows, a bound that some block reaches; the two entries of a row differ.
All inputs are finite; a program needn't handle non-finite values.
Results may differ from a plain program's by a relative error of at most 0.04.
Values may be sent and summed in bfloat16 or wider, within the bound.
A program may use at most 64 MiB of HBM per device.

v0:
```python
from functools import partial

import jax
import jax.numpy as jnp
from jax import lax
from jax.sharding import PartitionSpec as P

epsilon = 1e-05


def shifted(value, axis, steps):
    count = lax.axis_size(axis)
    initial, last = (max(0, -steps), min(count, count - steps))
    return lax.ppermute(value, axis, [(source, source + steps) for source in range(initial, last)])


def rms_scale(values, scale_gain):
    mean_square = jnp.mean(values * values, axis=-1, keepdims=True)
    return values * lax.rsqrt(mean_square + epsilon) * scale_gain


def slot_tables(block_routes, experts, capacity):
    count_rows = block_routes.shape[0]
    flat_routes = block_routes.reshape(-1)
    expert_hot = (flat_routes[:, None] == jnp.arange(experts, dtype=jnp.int32)[None, :]).astype(
        jnp.int32
    )
    earlier = jnp.cumsum(expert_hot, axis=0) - expert_hot
    slot_number = jnp.sum(earlier * expert_hot, axis=1)
    slot_hot = (slot_number[:, None] == jnp.arange(capacity, dtype=jnp.int32)[None, :]).astype(
        jnp.float32
    )
    return (
        expert_hot.astype(jnp.float32).reshape(count_rows, 2, experts),
        slot_hot.reshape(count_rows, 2, capacity),
    )


def shards(
    tokens, routes, w_router, norm_gain, w_gate, w_up, w_down, final_gain, head_weights, vocab_proj
):
    highest = lax.Precision.HIGHEST
    n_blocks = lax.axis_size("dp")
    block_index = lax.axis_index("dp")
    owner_index = lax.axis_index("expert")
    tok_rows, width = tokens.shape
    experts = w_router.shape[1]
    capacity = min(tok_rows, 4 * tok_rows // experts)
    heads_count = head_weights.shape[0]
    col_width = head_weights.shape[2]
    tokens_f32 = tokens.astype(jnp.float32)
    normed = rms_scale(tokens_f32, norm_gain).astype(jnp.bfloat16)
    router = jnp.dot(normed, w_router, preferred_element_type=jnp.float32)
    own_routes = lax.dynamic_slice_in_dim(routes, block_index * tok_rows, tok_rows, 0)
    expert_hot, slot_hot = slot_tables(own_routes, experts, capacity)
    chosen = jnp.sum(router[:, None, :] * expert_hot, axis=-1)
    first = jax.nn.sigmoid(chosen[:, 0] - chosen[:, 1])
    gates = jnp.stack([first, 1.0 - first], axis=1)
    my_expert = owner_index // 2
    weighted = jnp.einsum("tje,tjs,tj->est", expert_hot, slot_hot, gates, precision=highest)
    my_weighted = lax.dynamic_index_in_dim(weighted, my_expert, 0, keepdims=False)
    gate_half = w_gate[0]
    up_half = w_up[0]
    down_half = w_down[0]
    everyone = lax.all_gather(normed, "dp", axis=0, tiled=True)
    tables = jax.vmap(partial(slot_tables, experts=experts, capacity=capacity))
    all_expert, all_slot = tables(routes.reshape(n_blocks, tok_rows, 2))
    picked = lax.dynamic_index_in_dim(all_expert, my_expert, 3, keepdims=False)
    select = jnp.einsum("btj,btjs->bst", picked, all_slot).astype(jnp.bfloat16)
    gathered_rows = jnp.einsum(
        "bst,btd->bsd",
        select,
        everyone.reshape(n_blocks, tok_rows, width),
        preferred_element_type=jnp.float32,
    )
    gathered_rows = gathered_rows.astype(jnp.bfloat16).reshape(n_blocks * capacity, width)
    gate_pre = jnp.dot(gathered_rows, gate_half, preferred_element_type=jnp.float32)
    up_pre = jnp.dot(gathered_rows, up_half, preferred_element_type=jnp.float32)
    hidden = (jax.nn.silu(gate_pre) * up_pre).astype(jnp.bfloat16)
    partial_rows = jnp.dot(hidden, down_half, preferred_element_type=jnp.float32)
    slot_out = lax.psum_scatter(
        partial_rows.astype(jnp.bfloat16), "dp", scatter_dimension=0, tiled=True
    ).astype(jnp.float32)
    term = jnp.einsum("st,sd->td", my_weighted, slot_out, precision=highest)
    mixture = lax.psum(term.astype(jnp.bfloat16), "expert").astype(jnp.float32)
    final = rms_scale(tokens_f32 + mixture, final_gain).astype(jnp.bfloat16)
    vocab_all = lax.all_gather(vocab_proj, "dp", axis=0, tiled=True)
    teacher = jnp.dot(final, vocab_all, preferred_element_type=jnp.float32)
    teacher_total = lax.psum(jnp.sum(jnp.exp(teacher), axis=-1), "expert")
    teacher_logp = teacher - jnp.log(teacher_total)[:, None]
    following = shifted(teacher_logp[:heads_count], "dp", -1)
    extended = jnp.concatenate([teacher_logp, following], axis=0)
    preact = jnp.einsum(
        "tr,hrc->htc",
        final,
        lax.all_gather(head_weights, "dp", axis=1, tiled=True),
        preferred_element_type=jnp.float32,
    )
    own_columns = lax.dynamic_slice_in_dim(final, owner_index * col_width, col_width, 1).astype(
        jnp.float32
    )
    shares = (own_columns[None] + jax.nn.silu(preact)).astype(jnp.bfloat16)
    student_in = lax.all_gather(shares, "expert", axis=2, tiled=True)
    student = jnp.einsum("htd,dv->htv", student_in, vocab_all, preferred_element_type=jnp.float32)
    student_total = lax.psum(jnp.sum(jnp.exp(student), axis=-1), "expert")
    student_logp = student - jnp.log(student_total)[..., None]
    targets = jnp.stack(
        [
            extended[offset_index + 1 : offset_index + 1 + tok_rows]
            for offset_index in range(heads_count)
        ]
    )
    positions = block_index * tok_rows + jnp.arange(tok_rows, dtype=jnp.int32)
    total_rows = n_blocks * tok_rows
    steps_ahead = jnp.arange(1, heads_count + 1, dtype=jnp.int32)
    valid = (positions[None, :] + steps_ahead[:, None] < total_rows).astype(jnp.float32)
    row_weight = valid / (total_rows - steps_ahead).astype(jnp.float32)[:, None]
    probs = jnp.exp(targets)
    divergence = jnp.sum(probs * (targets - student_logp), axis=-1)
    head_losses = lax.psum(jnp.sum(row_weight * divergence, axis=-1), ("expert", "dp"))
    slopes = (row_weight[..., None] * (jnp.exp(student_logp) - probs)).astype(jnp.bfloat16)
    back_part = jnp.einsum("htv,dv->htd", slopes, vocab_all, preferred_element_type=jnp.float32)
    back_full = lax.psum(back_part.astype(jnp.bfloat16), "expert").astype(jnp.float32)
    back_cols = lax.dynamic_slice_in_dim(back_full, owner_index * col_width, col_width, 2)
    sigma = jax.nn.sigmoid(preact)
    pre_grad = (back_cols * sigma * (1.0 + preact * (1.0 - sigma))).astype(jnp.bfloat16)
    grad_all = lax.all_gather(pre_grad, "dp", axis=1, tiled=True)
    hidden_rows = lax.all_to_all(final, "dp", split_axis=1, concat_axis=0, tiled=True)
    head_grads = jnp.einsum(
        "tr,htc->hrc", hidden_rows, grad_all, preferred_element_type=jnp.float32
    )
    return (head_losses, head_grads)


def solution(mesh):
    in_specs = (
        P("dp", None),
        P(),
        P(),
        P(),
        P("expert", None, "dp"),
        P("expert", None, "dp"),
        P("expert", "dp", None),
        P(),
        P(None, "dp", "expert"),
        P("dp", "expert"),
    )
    out_specs = (P(), P(None, "dp", "expert"))
    return jax.shard_map(shards, mesh=mesh, in_specs=in_specs, out_specs=out_specs, check_vma=False)
```

profile of v0, /device:TPU:1, one launch (start us, length us, event | category | flops | bytes accessed | tf_op | source)
XLA Modules:
  0.0 821.5 jit_solution(17966482424876038804)
XLA Ops:
  8.4 1.7 fusion.23
  12.4 1.3 select_reduce_fusion
  13.9 4.3 fusion.14
  20.5 82.4 %all-gather.5.cloned.1.call-done = bf16[768,3072]{1,0:T(8,128)(2,1)} async-done(((bf16[24,3072]{1,0:T(8,128)(2,1)}), bf16[768,3072]{1,0:T(8,128)(2,1)}) %all-gather.5.cloned.1.call-update) | async-done | bytes 4718608 | tf_op jit(solution)/shard_map/all_gather | solution.py:65
  102.9 5.1 convolution_convert_fusion
  108.0 2.8 reshape.120
  110.8 1.9 fusion.18
  112.7 5.2 convolution_convert_fusion.1
  117.9 75.3 %fusion = bf16[16,3072]{1,0:T(8,128)(2,1)S(1)} fusion(bf16[384,3072]{1,0:T(8,128)(2,1)} %convolution_convert_fusion.1), kind=kCustom, calls=%all-reduce-scatter | all-reduce-scatter fusion | flops 1572865 | bytes 2459648
  193.2 1.5 collective-permute-start.1
  199.8 6.0 collective-permute-start.3
  205.8 6.9 collective-permute-start.4
  212.7 2.2 collective-permute-start.5
  214.9 3.7 collective-permute-start.6
  218.6 2.3 collective-permute-start.7
  221.0 1.6 collective-permute-done.7
  222.5 2.1 concatenate.4
  226.9 124.4 %all-reduce.6.cloned.1.call-done = bf16[24,3072]{1,0:T(8,128)(2,1)} async-done(((bf16[24,3072]{1,0:T(8,128)(2,1)}), bf16[24,3072]{1,0:T(8,128)(2,1)}) %all-reduce.6.cloned.1.call-update) | async-done | bytes 147472 | tf_op jit(solution)/shard_map/psum | solution.py:85
  353.5 93.7 %all-gather.9.cloned.1.call-done = bf16[4,3072,192]{2,1,0:T(8,128)(2,1)} async-done(((bf16[4,96,192]{2,1,0:T(8,128)(2,1)}), bf16[4,3072,192]{2,1,0:T(8,128)(2,1)}) %all-gather.9.cloned.1.call-update) | async-done | bytes 4718608 | tf_op jit(solution)/shard_map/all_gather | solution.py:96
  447.3 3.7 add_convert_fusion
  451.2 29.8 %all_gather.18 = bf16[4,24,3072]{1,0,2:T(4,128)(2,1)} all-gather(bf16[4,24,192]{1,0,2:T(4,128)(2,1)S(1)} %copy.63), channel_id=1, replica_groups=mesh['expert'=16,'dp'=32] {'expert'}, dimensions={2}, use_global_device_ids=true | all-gather | bytes 626688 | tf_op jit(solution)/shard_map/all_gather | solution.py:103
  480.9 60.3 %all-gather.7.cloned.1.call-done = bf16[3072,1024]{1,0:T(8,128)(2,1)} async-done(((bf16[96,1024]{1,0:T(8,128)(2,1)}), bf16[3072,1024]{1,0:T(8,128)(2,1)}) %all-gather.7.cloned.1.call-update) | async-done | bytes 6291472 | tf_op jit(solution)/shard_map/all_gather | solution.py:87
  541.2 4.0 exponential_reduce_fusion.1
  545.8 3.2 exponential_reduce_fusion
  549.0 24.1 %all-reduce.2 = (f32[24]{0:T(128)S(1)}, f32[4,24]{1,0:T(4,128)S(1)}) all-reduce(f32[24]{0:T(128)S(1)} %get-tuple-element.24, f32[4,24]{1,0:T(4,128)S(1)} %get-tuple-element.26), channel_id=1, replica_groups=mesh['expert'=16,'dp'=32] {'expert'}, use_global_device_ids=true, to_apply=%region_10.11 | all-reduce | flops 120 | bytes 960 | tf_op jit(solution)/shard_map/psum | solution.py:89
  574.5 3.2 collective-permute-done
  578.1 5.7 fusion.5
  583.9 115.1 %all-reduce.8.cloned.1.call-done = bf16[4,24,3072]{2,1,0:T(8,128)(2,1)} async-done(((bf16[4,24,3072]{2,1,0:T(8,128)(2,1)}), bf16[4,24,3072]{2,1,0:T(8,128)(2,1)}) %all-reduce.8.cloned.1.call-update) | async-done | bytes 589840 | tf_op jit(solution)/shard_map/psum | solution.py:123
  699.0 1.6 multiply_convert_fusion.3
  701.6 9.9 %all-to-all-start = ((bf16[24,32,96]{2,0,1:T(8,128)(2,1)}), bf16[24,32,96]{2,0,1:T(8,128)(2,1)S(1)}, u32[]{:S(2)}, u32[]{:S(2)}) async-start(bf16[24,32,96]{2,0,1:T(8,128)(2,1)} %copy.65), calls=%async_computation | async-start | bytes 393216 | tf_op jit(solution)/shard_map/all_to_all | solution.py:128
  711.5 100.2 %psum.38 = f32[4]{0:T(128)} all-reduce(f32[4]{0:T(128)S(1)} %get-tuple-element.21), channel_id=1, replica_groups=mesh['expert'=16,'dp'=32] {'expert','dp'}, use_global_device_ids=true, to_apply=%region_15.16 | all-reduce | flops 4 | bytes 32 | tf_op jit(solution)/shard_map/psum | solution.py:120
  811.7 2.0 convolution_bitcast_fusion
  (80 shorter events, 19.3 us)
Async XLA Ops:
  7.2 105.6 %copy-start = (bf16[1,128,3072]{2,1,0:T(8,128)(2,1)S(1)}, bf16[1,128,3072]{2,1,0:T(8,128)(2,1)}, u32[]{:S(2)}) copy-start(bf16[1,128,3072]{2,1,0:T(8,128)(2,1)} %param.16) | copy-start | bytes 2359300
  7.2 12.8 %copy-start.4 = (bf16[3072,8]{0,1:T(8,128)(2,1)S(1)}, bf16[3072,8]{0,1:T(8,128)(2,1)}, u32[]{:S(2)}) copy-start(bf16[3072,8]{0,1:T(8,128)(2,1)} %param.12) | copy-start | bytes 147460
  7.2 95.7 %all-gather.5.cloned.1.call-start = ((), (), s32[]{:S(2)}) async-start(), calls=%async_computation.1 | async-start | bytes 4866048 | tf_op jit(solution)/shard_map/all_gather | solution.py:65
  10.0 9.9 %copy-start.3 = (bf16[24,3072]{1,0:T(8,128)(2,1)S(1)}, bf16[24,3072]{1,0:T(8,128)(2,1)}, u32[]{:S(2)}) copy-start(bf16[24,3072]{1,0:T(8,128)(2,1)} %fusion.23) | copy-start | bytes 442372
  10.1 341.3 %all-reduce.6.cloned.1.call-start = ((), (), s32[]{:S(2)}) async-start(), calls=%async_computation.2 | async-start | bytes 294912 | tf_op jit(solution)/shard_map/psum | solution.py:85
  117.9 233.5 %copy-start.2 = (bf16[24,3072]{1,0:T(8,128)(2,1)S(1)}, bf16[24,3072]{1,0:T(8,128)(2,1)}, u32[]{:S(2)}) copy-start(bf16[24,3072]{1,0:T(8,128)(2,1)} %param.10) | copy-start | bytes 442372
  117.9 234.5 %copy-start.5 = (f32[3072]{0:T(1024)S(1)}, f32[3072]{0:T(1024)}, u32[]{:S(2)}) copy-start(f32[3072]{0:T(1024)} %param.17) | copy-start | bytes 36868
  193.2 21.7 %collective-permute-start.1 = (bf16[16,3072]{1,0:T(8,128)(2,1)S(1)}, bf16[16,3072]{1,0:T(8,128)(2,1)S(1)}, u32[]{:S(2)}, u32[]{:S(2)}) collective-permute-start(bf16[16,3072]{1,0:T(8,128)(2,1)S(1)} %fusion), channel_id=1, source_target_pairs={{0,1},{1,2},{2,3},{3,4},{4,5},{5,6},{6,7},{7,8},{8,9},{9,10},{10,1... | collective-permute-start | bytes 294920
  194.7 23.9 %collective-permute-start.2 = (bf16[16,3072]{1,0:T(8,128)(2,1)S(1)}, bf16[16,3072]{1,0:T(8,128)(2,1)S(1)}, u32[]{:S(2)}, u32[]{:S(2)}) collective-permute-start(bf16[16,3072]{1,0:T(8,128)(2,1)S(1)} %fusion), channel_id=1, source_target_pairs={{0,2},{1,3},{2,4},{3,5},{4,6},{5,7},{6,8},{7,9},{8,10},{9,11},{10,... | collective-permute-start | bytes 294920
  196.0 16.6 %collective-permute-start.8 = (bf16[12,3072]{1,0:T(8,128)(2,1)S(1)}, bf16[12,3072]{1,0:T(8,128)(2,1)S(1)}, u32[]{:S(2)}, u32[]{:S(2)}) collective-permute-start(bf16[12,3072]{1,0:T(8,128)(2,1)S(1)} %slice.37), channel_id=1, source_target_pairs={{0,8},{1,9},{2,10},{3,11},{4,12},{5,13},{6,14},{7,15},{8,16},{9,17... | collective-permute-start | bytes 221192
  199.8 21.1 %collective-permute-start.3 = (bf16[16,3072]{1,0:T(8,128)(2,1)S(1)}, bf16[16,3072]{1,0:T(8,128)(2,1)S(1)}, u32[]{:S(2)}, u32[]{:S(2)}) collective-permute-start(bf16[16,3072]{1,0:T(8,128)(2,1)S(1)} %fusion), channel_id=1, source_target_pairs={{0,3},{1,4},{2,5},{3,6},{4,7},{5,8},{6,9},{7,10},{8,11},{9,12},{10... | collective-permute-start | bytes 294920
  205.8 15.1 %collective-permute-start.4 = (bf16[16,3072]{1,0:T(8,128)(2,1)S(1)}, bf16[16,3072]{1,0:T(8,128)(2,1)S(1)}, u32[]{:S(2)}, u32[]{:S(2)}) collective-permute-start(bf16[16,3072]{1,0:T(8,128)(2,1)S(1)} %fusion), channel_id=1, source_target_pairs={{0,4},{1,5},{2,6},{3,7},{4,8},{5,9},{6,10},{7,11},{8,12},{9,13},{1... | collective-permute-start | bytes 294920
  212.7 8.3 %collective-permute-start.5 = (bf16[16,3072]{1,0:T(8,128)(2,1)S(1)}, bf16[16,3072]{1,0:T(8,128)(2,1)S(1)}, u32[]{:S(2)}, u32[]{:S(2)}) collective-permute-start(bf16[16,3072]{1,0:T(8,128)(2,1)S(1)} %fusion), channel_id=1, source_target_pairs={{0,5},{1,6},{2,7},{3,8},{4,9},{5,10},{6,11},{7,12},{8,13},{9,14},{... | collective-permute-start | bytes 294920
  214.9 6.0 collective-permute-start.6
  218.6 3.9 collective-permute-start.7
  225.6 221.7 %all-gather.9.cloned.1.call-start = ((), (), s32[]{:S(2)}) async-start(), calls=%async_computation.4 | async-start | bytes 6488064 | tf_op jit(solution)/shard_map/all_gather | solution.py:96
  226.3 314.9 %all-gather.7.cloned.1.call-start = ((), (), s32[]{:S(2)}) async-start(), calls=%async_computation.3 | async-start | bytes 6488064 | tf_op jit(solution)/shard_map/all_gather | solution.py:87
  226.9 472.2 %all-reduce.8.cloned.1.call-start = ((), (), s32[]{:S(2)}) async-start(), calls=%async_computation.5 | async-start | bytes 1179648 | tf_op jit(solution)/shard_map/psum | solution.py:123
  541.2 4.6 copy-start.1
  573.2 4.5 collective-permute-start
  583.9 227.8 %all-gather.11.cloned.1.call-start = ((), (), s32[]{:S(2)}) async-start(), calls=%async_computation.6 | async-start | bytes 1622016 | tf_op jit(solution)/shard_map/all_gather | solution.py:127
  701.6 110.1 %all-to-all-start = ((bf16[24,32,96]{2,0,1:T(8,128)(2,1)}), bf16[24,32,96]{2,0,1:T(8,128)(2,1)S(1)}, u32[]{:S(2)}, u32[]{:S(2)}) async-start(bf16[24,32,96]{2,0,1:T(8,128)(2,1)} %copy.65), calls=%async_computation | async-start | bytes 393216 | tf_op jit(solution)/shard_map/all_to_all | solution.py:128
Sparse Core Ops, SparseCore 0:
  11.7 91.0 all-gather.4
  225.7 125.6 all-reduce.5
  354.5 92.6 all-gather.8
  450.3 90.8 all-gather.6
  584.0 115.0 all-reduce.7
  702.1 79.0 all-gather.10
where the time goes:
time: 823 us; the launch traced here: 822 us
  waiting for transfers between devices  482 us (59%)
  blocking collectives  229 us (28%)
  starting transfers between devices  36.6 us (4%)
  matrix products  32.4 us (4%)
  between operations  15.2 us (2%)
  other arithmetic  13.4 us (2%)
  local copies, waits for them, and re-layouts  12.7 us (2%)
    psum x1, waiting for transfers between devices, shards(): mixture = lax.psum(term.astype(jnp.bfloat16), 'expert').astype(jnp.float32)  124 us
    psum x1, waiting for transfers between devices, shards(): lax.psum(back_part.astype(jnp.bfloat16), 'expert').astype(jnp.float32)  115 us
    psum x1, blocking collectives, shards(): lax.psum(jnp.sum(row_weight * divergence, axis=-1), ('expert', 'dp'))  100 us
    all_gather x1, waiting for transfers between devices, shards(): lax.all_gather(head_weights, 'dp', axis=1, tiled=True)  93.7 us
    all_gather x1, waiting for transfers between devices, shards(): everyone = lax.all_gather(normed, 'dp', axis=0, tiled=True)  82.4 us
    unnamed x1, blocking collectives  75.3 us
    all_gather x1, waiting for transfers between devices, shards(): vocab_all = lax.all_gather(vocab_proj, 'dp', axis=0, tiled=True)  60.3 us
    all_gather x1, blocking collectives, shards(): student_in = lax.all_gather(shares, 'expert', axis=2, tiled=True)  29.8 us
  transfers between devices with their start and end apart: 16, of which 7 were waited for; matrix products, arithmetic and copies ran while one was open for 2% of the time, Pallas kernels for 0%

commit v1 on v0

v1 whole, which is shorter than its diff:
```python
import jax
import jax.numpy as jnp
from jax import lax
from jax.experimental import pallas as pl
from jax.experimental.pallas import tpu as pltpu
from jax.sharding import PartitionSpec as P

MESH = pl.DeviceIdType.MESH
F32, BF16 = jnp.float32, jnp.bfloat16
HIGHEST = lax.Precision.HIGHEST
EPS = 1e-05
NX = 4
TOK, CAP, SLOT = 24, 12, 16
N_COPIES = 190


def dot(a, b, dims=((1,), (0,)), precision=None):
    return lax.dot_general(a, b, (dims, ((), ())), precision=precision, preferred_element_type=F32)


def iota(shape, axis):
    return lax.broadcasted_iota(jnp.int32, shape, axis)


def one_hot(rows, cols, group, pitch):
    row = iota((rows, cols), 0)
    target = row
    for start in range(group, rows, group):
        target = target + jnp.where(row >= start, pitch - group, 0)
    return (target == iota((rows, cols), 1)).astype(BF16)


def spread(rows, cols, group, pitch):
    col = iota((rows, cols), 1)
    target = col
    for start in range(group, cols, group):
        target = target + jnp.where(col >= start, pitch - group, 0)
    return (target == iota((rows, cols), 0)).astype(BF16)


class Ring:
    def __init__(self, copy, n, me, plus, minus):
        self.copy, self.n, self.me, self.plus, self.minus = copy, n, me, plus, minus

    def at(self, offset):
        return lax.rem(self.me + (offset + self.n), self.n)


def body(
    nz, ny, tok_ref, routes_ref, wr_ref, ng_ref, fg_ref, hw_ref, wg_hbm, wu_hbm, wd_hbm, voc_hbm, loss_ref, out_ref,
    w_gu, wd, vg, hx, hl, hg, nbs, ax, ag, po, ps, pr, dl, rl, dr, rr, xs, xr, yg, sq, fp, f96, fw, fn, gfac, sg,
    ls, tl, sums, lsum, sl, bo, bs, br, el, erl, er, err, xs2, xr2, gg, osd, ord_, oown, r1, r2, q1, q2, q3,
    ss, rs, lsem,
):
    dp, ex = lax.axis_index("dp"), lax.axis_index("expert")
    z, x = lax.div(dp, NX), lax.rem(dp, NX)
    y, c = lax.div(ex, 2), lax.rem(ex, 2)
    oc = 1 - c
    d_model = tok_ref.shape[1]
    half = d_model // 2
    vcols = vg.shape[2]
    kcols = d_model // ny
    zrows = d_model // nz
    grp = NX * TOK
    hrow = grp // 2

    def dev(z_=None, x_=None, y_=None, c_=None):
        z_, x_ = (z if z_ is None else z_), (x if x_ is None else x_)
        y_, c_ = (y if y_ is None else y_), (c if c_ is None else c_)
        return {"dp": z_ * NX + x_, "expert": y_ * 2 + c_}

    def xo(d):
        return lax.rem(x + d, NX)

    def zo(d):
        return lax.rem(z + (d + nz), nz)

    def yo(d):
        return lax.rem(y + (d + ny), ny)

    partner = dev(c_=oc)
    sent = []

    def copy(src, dst, device):
        i = len(sent)
        cp = pltpu.make_async_remote_copy(
            src_ref=src, dst_ref=dst, send_sem=ss.at[i], recv_sem=rs.at[i], device_id=device, device_id_type=MESH
        )
        cp.start()
        sent.append(cp)
        return cp

    locals_ = []

    def local(src, dst):
        cp = pltpu.make_async_copy(src, dst, lsem.at[len(locals_)])
        cp.start()
        locals_.append(cp)
        return cp

    def arrive(copies):
        for cp in copies:
            cp.wait_recv()

    quarter = lambda x_: pl.ds(pl.multiple_of(x_ * vcols, 128), vcols)
    hcols = lambda c_: pl.ds(pl.multiple_of(c_ * half, 128), half)
    in_w = [
        local(wg_hbm, w_gu.at[:, 0:128]),
        local(wu_hbm, w_gu.at[:, 128:256]),
        local(wd_hbm.at[:, hcols(c)], wd.at[0]),
        local(wd_hbm.at[:, hcols(oc)], wd.at[1]),
    ]
    vrow = 96
    vslot = lambda x_: pl.ds(pl.multiple_of(x_ * vrow, 16), vrow)
    in_v = local(voc_hbm.at[:, quarter(x)], vg.at[z, vslot(x), :])

    barrier = pltpu.get_barrier_semaphore()
    line_z = [dev(z_=zo(d)) for d in range(1, nz)]
    line_y = [dev(y_=yo(d)) for d in range(1, ny)]
    near = [(xo(d), c_) for d in range(1, NX) for c_ in (c, oc)] + [(x, oc)]
    plane = [dev(x_=a, c_=b) for a, b in near]
    peers = line_z + line_y + plane
    for peer in peers:
        pl.semaphore_signal(barrier, inc=1, device_id=peer, device_id_type=MESH)

    tok = tok_ref[...].astype(F32)
    mean_square = jnp.sum(tok * tok, axis=-1, keepdims=True) * (1.0 / d_model)
    normed = (tok * lax.rsqrt(mean_square + EPS) * ng_ref[...]).astype(BF16)
    nbs[0] = normed[:, :half]
    nbs[1] = normed[:, half:]
    router = dot(normed, wr_ref[...], ((1,), (1,)))
    own_routes = routes_ref[pl.ds(pl.multiple_of(dp * TOK, 8), TOK), :]
    r0, r1_ = own_routes[:, 0:1], own_routes[:, 1:2]
    n_exp = router.shape[1]
    lane_e = iota((TOK, n_exp), 1)
    hot0, hot1 = (r0 == lane_e).astype(F32), (r1_ == lane_e).astype(F32)
    lower = (iota((TOK, TOK), 1) < iota((TOK, TOK), 0)).astype(BF16)
    earlier = dot(lower, (hot0 + hot1).astype(BF16))
    place0 = r0.astype(F32) * SLOT + jnp.sum(hot0 * earlier, axis=1, keepdims=True)
    place1 = r1_.astype(F32) * SLOT + jnp.sum(hot1 * earlier, axis=1, keepdims=True)
    first = jax.nn.sigmoid(jnp.sum(router * (hot0 - hot1), axis=1, keepdims=True))
    lane_f = iota((TOK, n_exp * SLOT), 1).astype(F32)
    weigh = first * (place0 == lane_f).astype(F32) + (1.0 - first) * (place1 == lane_f).astype(F32)
    weigh_hi = weigh.astype(BF16)
    weigh_lo = (weigh - weigh_hi.astype(F32)).astype(BF16)
    own_slot = (iota((TOK, SLOT), 1) + y * SLOT).astype(F32)
    select = ((place0 == own_slot).astype(F32) + (place1 == own_slot).astype(F32)).astype(BF16)
    ax[x] = dot(select, nbs[c], ((0,), (0,))).astype(BF16)

    pl.semaphore_wait(barrier, len(peers))

    def gather_ring(n, off, plus, minus, at, on_arrival):
        on_arrival(off(0))
        arrived = None
        for s in range(1, n // 2 + 1):
            a = copy(at(off(-(s - 1))), at(off(-(s - 1))), plus)
            b = copy(at(off(s - 1)), at(off(s - 1)), minus) if s < n // 2 else None
            yield
            a.wait_recv()
            on_arrival(off(-s))
            if b is not None:
                b.wait_recv()
                on_arrival(off(s))
        yield

    def run(gen):
        for _ in gen:
            pass

    nothing = lambda i: None

    def background():
        vx = [copy(voc_hbm.at[:, quarter(xo(d))], vg.at[z, vslot(x), :], dev(x_=xo(d))) for d in range(1, NX)]
        rows = lambda c_: pl.ds(pl.multiple_of(c_ * hrow, 16), hrow)
        ex_h = copy(hw_ref.at[:, rows(oc), :], hx, partner)
        yield
        ex_h.wait_recv()
        for k in range(NX):
            mine, theirs = hw_ref[k, rows(c), :], hx[k]
            left = jnp.where(c == 0, mine, theirs)
            right = jnp.where(c == 0, theirs, mine)
            hl[k] = jnp.concatenate([left, right], axis=1)
        hxc = [copy(hl.at[xo(d)], hg.at[z, x, c], dev(x_=xo(d))) for d in range(1, NX)]
        hg[z, x, c] = hl[x]
        yield
        arrive(hxc)
        forwards = []

        def forward(i):
            forwards.append(copy(hg.at[i, :, c], hg.at[i, :, c], partner))

        yield from gather_ring(nz, zo, dev(z_=zo(1)), dev(z_=zo(-1)), lambda i: hg.at[i, :, c], forward)
        arrive(forwards)
        yield "heads"
        arrive(vx)
        in_v.wait()
        yield from gather_ring(nz, zo, dev(z_=zo(1)), dev(z_=zo(-1)), lambda i: vg.at[i], nothing)

    bg = background()

    def step(n=1):
        for _ in range(n):
            next(bg, None)

    step()
    arrive([copy(ax.at[x], ax.at[x], dev(x_=xo(d))) for d in range(1, NX)])
    pick = one_hot(NX * CAP, NX * SLOT, CAP, SLOT)
    ag[c, z] = dot(pick, ax[...].reshape(NX * SLOT, half)).astype(BF16)
    step()
    fwd = []

    def forward_a(i):
        fwd.append(copy(ag.at[c, i], ag.at[c, i], partner))

    run(gather_ring(nz, zo, dev(z_=zo(1)), dev(z_=zo(-1)), lambda i: ag.at[c, i], forward_a))
    step()
    arrive(fwd)
    for cp in in_w:
        cp.wait()

    n_rows = nz * NX * CAP
    pre = dot(ag[0].reshape(n_rows, half), w_gu[:half, :]) + dot(ag[1].reshape(n_rows, half), w_gu[half:, :])
    gate, up = pre[:, :128], pre[:, 128:]
    hidden = (jax.nn.silu(gate) * up).astype(BF16)
    ps[...] = dot(hidden, wd[1]).astype(BF16).reshape(ps.shape)
    order = [4, 3, -3, 2, -2, 1, -1, 0]
    got = {}
    for o in order:
        got[o] = copy(ps.at[zo(o)], pr.at[zo(o)], partner)
    po[...] = dot(hidden, wd[0]).reshape(po.shape)
    step()

    def scatter_ring(n, off, plus, minus, own, got, left, in_left, right, in_right, between):
        h = n // 2
        a = b = None
        seen = set()

        def term(o):
            o = -h if o == h else o
            key = h if o == -h else o
            if key not in seen:
                got[key].wait_recv()
                seen.add(key)
            return own(off(o))

        for s in range(1, h + 1):
            value = term(-(h + 1 - s))
            if a is not None:
                a.wait_recv()
                value = value + in_left[s - 2].astype(F32)
            left[s - 1] = value.astype(BF16)
            a = copy(left.at[s - 1], in_left.at[s - 1], minus)
            if s < h:
                value = term(h - s)
                if b is not None:
                    b.wait_recv()
                    value = value + in_right[s - 2].astype(F32)
                right[s - 1] = value.astype(BF16)
                b = copy(right.at[s - 1], in_right.at[s - 1], plus)
            between()
        value = term(0)
        b.wait_recv()
        value = value + in_right[h - 2].astype(F32)
        a.wait_recv()
        return value + in_left[h - 1].astype(F32)

    total = scatter_ring(
        nz, zo, dev(z_=zo(1)), dev(z_=zo(-1)), lambda i: po[i] + pr[i].astype(F32), got, dl, rl, dr, rr, lambda: None
    )
    step()
    place = spread(NX * SLOT, NX * CAP, CAP, SLOT)
    xs[...] = dot(place, total.astype(BF16)).astype(BF16).reshape(xs.shape)
    arrive([copy(xs.at[xo(d)], xr.at[x], dev(x_=xo(d))) for d in range(1, NX)])
    rows = xs[x].astype(F32)
    for d in range(1, NX):
        rows = rows + xr[xo(d)].astype(F32)
    yg[y] = rows.astype(BF16)

    ycp = [copy(yg.at[y], yg.at[y], dev(y_=yo(d))) for d in range(1, ny)]
    step()
    arrive(ycp)
    outs = yg[...].reshape(ny * SLOT, half)
    mixed = tok_ref[:, hcols(c)].astype(F32) + dot(weigh_hi, outs) + dot(weigh_lo, outs)
    square = jnp.sum(mixed * mixed, axis=1, keepdims=True)
    sq[0] = jnp.broadcast_to(square, (TOK, 128))
    scp = copy(sq.at[0], sq.at[1], partner)
    scp.wait_recv()
    mean_square = (square + sq[1][:, 0:1]) * (1.0 / d_model)
    fin = (mixed * lax.rsqrt(mean_square + EPS) * fg_ref[:, hcols(c)]).astype(BF16)
    fp[c, x] = dot(spread(32, TOK, TOK, TOK), fin).astype(BF16)
    fcp = [copy(fp.at[c, x], fp.at[c, x], dev(x_=xo(d))) for d in range(1, NX)]
    fwd = [copy(fp.at[c, x], fp.at[c, x], partner)]
    for d, cp in zip(range(1, NX), fcp):
        cp.wait_recv()
        src = xo(NX - d)
        fwd.append(copy(fp.at[c, src], fp.at[c, src], partner))
    step()
    arrive(fwd)
    pick = one_hot(grp, NX * 32, TOK, 32)
    for h in range(2):
        f96[:, h * half : (h + 1) * half] = dot(pick, fp[h].reshape(NX * 32, half)).astype(BF16)

    hrows = pl.ds(pl.multiple_of(c * hrow, 16), hrow)

    def window(z_):
        start = jnp.minimum(lax.div((z_ * NX + x) * vrow, 128) * 128, d_model - 256)
        return pl.ds(pl.multiple_of(start, 128), 256)

    tcp = [copy(f96.at[hrows, window(zo(d))], fw.at[z], dev(z_=zo(d))) for d in range(1, nz)]
    fw[z] = f96[hrows, window(z)]
    ncp = copy(f96.at[0:16, :], fn, dev(z_=zo(-1)))

    while next(bg, "heads") != "heads":
        pass
    ycols = lambda y_: pl.ds(pl.multiple_of(y_ * kcols, 128), kcols)
    preact = dot(f96[hrows, :], hg[...].reshape(d_model, kcols))
    sigma = jax.nn.sigmoid(preact)
    gfac[...] = sigma * (1.0 + preact * (1.0 - sigma))
    student = f96[hrows, ycols(y)].astype(F32) + preact * sigma
    sg[c, x, :, ycols(y)] = student.astype(BF16)
    step()
    arrive(
        [
            copy(sg.at[c, x, :, ycols(y)], sg.at[c, x, :, ycols(y)], dev(x_=xo(d)))
            for d in range(1, NX)
        ]
    )
    fwd = []

    def forward_s(i):
        fwd.append(copy(sg.at[c, :, :, ycols(i)], sg.at[c, :, :, ycols(i)], partner))

    for _ in gather_ring(ny, yo, dev(y_=yo(1)), dev(y_=yo(-1)), lambda i: sg.at[c, :, :, ycols(i)], forward_s):
        step()
    run(bg)
    ncp.wait_recv()
    voc = vg[...].reshape(d_model, vcols)
    logit_t = dot(f96[...], voc)
    logit_n = dot(fn[...], voc)
    arrive(fwd)
    n_st = NX * grp
    ls[0:n_st, :] = dot(sg[...].reshape(n_st, d_model), voc)
    ls[n_st : n_st + grp, :] = logit_t
    ls[n_st + grp : n_st + grp + 16, :] = logit_n
    ls[n_st + grp + 16 :, :] = jnp.zeros((16, vcols), F32)

    def reduce_plane(src, first_in, second_in):
        cps = [copy(src, first_in.at[x * 2 + c], dev(x_=a, c_=b)) for a, b in near]
        arrive(cps)
        row = src[...]
        for a, b in near:
            row = row + first_in[a * 2 + b]
        second_in[y] = row
        cps = [copy(second_in.at[y], second_in.at[y], dev(y_=yo(d))) for d in range(1, ny)]
        arrive(cps)
        row = second_in[0]
        for i in range(1, ny):
            row = row + second_in[i]
        return row

    ones = jnp.ones((8, vcols), F32)
    sums[...] = dot(ones, jnp.exp(ls[...]), ((1,), (1,)), HIGHEST)[0:1, :]
    logs = jnp.log(reduce_plane(sums, r1, r2))
    n_all = ls.shape[0]
    first_row = (iota((8, 128), 0) == 0).astype(F32)
    column = dot(jnp.broadcast_to(logs, (8, n_all)), first_row, ((0,), (0,)), HIGHEST)[:, 0:1]
    tl[...] = ls[n_st : n_st + tl.shape[0], :] - column[n_st : n_st + tl.shape[0]]
    losses = [None] * NX
    row_id = iota((hrow, 1), 0)
    n_tok = nz * grp
    for h in range(2):
        for k in range(NX):
            at = (h * NX + k) * hrow
            logp = ls[at : at + hrow, :] - column[at : at + hrow]
            target = tl[h * hrow + k + 1 : h * hrow + k + 1 + hrow, :]
            p = jnp.exp(target)
            weight = jnp.where(z * grp + h * hrow + row_id + (k + 1) < n_tok, 1.0 / (n_tok - k - 1), 0.0)
            terms = jnp.sum(weight * (p * (target - logp)), axis=0, keepdims=True)
            losses[k] = terms if losses[k] is None else losses[k] + terms
            sl[h, k * hrow : (k + 1) * hrow, :] = (weight * (jnp.exp(logp) - p)).astype(BF16)
    for k in range(NX):
        lsum[:, k * 128 : (k + 1) * 128] = losses[k][:, :128] + losses[k][:, 128:]

    got = {}
    for o in order:
        bs[yo(o)] = dot(sl[oc], vg[yo(o)], ((1,), (1,))).astype(BF16)
        got[o] = copy(bs.at[yo(o)], br.at[yo(o)], partner)
    for o in order:
        bo[yo(o)] = dot(sl[c], vg[yo(o)], ((1,), (1,)))
    total = scatter_ring(
        ny, yo, dev(y_=yo(1)), dev(y_=yo(-1)), lambda i: bo[i] + br[i].astype(F32), got, el, erl, er, err, lambda: None
    )
    xs2[...] = total.astype(BF16).reshape(xs2.shape)
    bcp = [copy(xs2.at[xo(d)], xr2.at[x], dev(x_=xo(d))) for d in range(1, NX)]
    arrive(tcp)
    turned = fw[...].reshape(nz * hrow, 256).astype(F32).T.astype(BF16)
    arrive(bcp)
    back = xs2[x].astype(F32)
    for d in range(1, NX):
        back = back + xr2[xo(d)].astype(F32)
    gg[z, x] = (back * gfac[...]).astype(BF16)

    arrive([copy(gg.at[z, x], gg.at[z, x], dev(x_=xo(d))) for d in range(1, NX)])
    ring = gather_ring(nz, zo, dev(z_=zo(1)), dev(z_=zo(-1)), lambda i: gg.at[i], nothing)
    next(ring)
    q3[z] = reduce_plane(lsum, q1, q2)
    lcp = [copy(q3.at[z], q3.at[z], dev(z_=zo(d))) for d in range(1, nz)]
    run(ring)

    cut = dp * vrow - jnp.minimum(lax.div(dp * vrow, 128) * 128, d_model - 256)
    oown[...] = turned
    lhs = oown[pl.ds(pl.multiple_of(cut, 32), vrow), :]
    cols = kcols // 2
    keep = []
    for k in range(NX):
        o = dot(lhs, gg[:, k].reshape(nz * hrow, kcols))
        low, high = o[:, :cols], o[:, cols:]
        osd[k] = jnp.where(c == 0, high, low)
        out_ref[k] = jnp.where(c == 0, low, high)
    ocp = copy(osd, ord_, partner)
    arrive(lcp)
    row = q3[0]
    for i in range(1, nz):
        row = row + q3[i]
    for k in range(NX):
        loss_ref[k] = jnp.sum(row[:, k * 128 : (k + 1) * 128])
    ocp.wait_recv()
    out_ref[...] = out_ref[...] + ord_[...]
    for cp in sent:
        cp.wait_send()


def solution(mesh):
    nz, ny = mesh.shape["dp"] // NX, mesh.shape["expert"] // 2

    def shards(tokens, routes, w_router, norm_gain, w_gate, w_up, w_down, final_gain, head_weights, vocab_proj):
        d_model = tokens.shape[1]
        half = d_model // 2
        kcols = d_model // ny
        vcols = vocab_proj.shape[1] // NX
        grp = NX * TOK
        hrow = grp // 2
        slots = NX * CAP
        vm = pltpu.VMEM
        scratch = [
            vm((d_model, 256), BF16),
            vm((2, 128, half), BF16),
            vm((nz, d_model // nz, vcols), BF16),
            vm((NX, hrow, kcols // 2), BF16),
            vm((NX, hrow, kcols), BF16),
            vm((nz, NX, 2, hrow, kcols), BF16),
            vm((2, TOK, half), BF16),
            vm((NX, SLOT, half), BF16),
            vm((2, nz, slots, half), BF16),
            vm((nz, slots, half), F32),
            vm((nz, slots, half), BF16),
            vm((nz, slots, half), BF16),
            vm((nz // 2, slots, half), BF16),
            vm((nz // 2, slots, half), BF16),
            vm((nz // 2, slots, half), BF16),
            vm((nz // 2, slots, half), BF16),
            vm((NX, SLOT, half), BF16),
            vm((NX, SLOT, half), BF16),
            vm((ny, SLOT, half), BF16),
            vm((2, TOK, 128), F32),
            vm((2, NX, 32, half), BF16),
            vm((grp, d_model), BF16),
            vm((nz, hrow, 256), BF16),
            vm((16, d_model), BF16),
            vm((hrow, kcols), F32),
            vm((2, NX, hrow, d_model), BF16),
            vm((512, vcols), F32),
            vm((grp + 16, vcols), F32),
            vm((1, 512), F32),
            vm((1, 512), F32),
            vm((2, NX * hrow, vcols), BF16),
            vm((ny, NX * hrow, kcols), F32),
            vm((ny, NX * hrow, kcols), BF16),
            vm((ny, NX * hrow, kcols), BF16),
            vm((ny // 2, NX * hrow, kcols), BF16),
            vm((ny // 2, NX * hrow, kcols), BF16),
            vm((ny // 2, NX * hrow, kcols), BF16),
            vm((ny // 2, NX * hrow, kcols), BF16),
            vm((NX, hrow, kcols), BF16),
            vm((NX, hrow, kcols), BF16),
            vm((nz, NX, hrow, kcols), BF16),
            vm((NX, 96, kcols // 2), F32),
            vm((NX, 96, kcols // 2), F32),
            vm((256, nz * hrow), BF16),
            vm((2 * NX, 1, 512), F32),
            vm((ny, 1, 512), F32),
            vm((2 * NX, 1, 512), F32),
            vm((ny, 1, 512), F32),
            vm((nz, 1, 512), F32),
            pltpu.SemaphoreType.DMA((N_COPIES,)),
            pltpu.SemaphoreType.DMA((N_COPIES,)),
            pltpu.SemaphoreType.DMA((8,)),
        ]

        def kernel(*refs):
            body(nz, ny, *refs)

        in_vmem = pl.BlockSpec(memory_space=pltpu.VMEM)
        in_hbm = pl.BlockSpec(memory_space=pl.ANY)
        losses, grads = pl.pallas_call(
            kernel,
            out_shape=(
                jax.ShapeDtypeStruct((NX,), F32),
                jax.ShapeDtypeStruct((NX, 96, kcols // 2), F32),
            ),
            in_specs=[in_vmem] * 6 + [in_hbm] * 4,
            out_specs=(pl.BlockSpec(memory_space=pltpu.SMEM), in_vmem),
            scratch_shapes=scratch,
            compiler_params=pltpu.CompilerParams(
                collective_id=0, has_side_effects=True, vmem_limit_bytes=60 * 2**20
            ),
            name="step",
        )(
            tokens,
            routes,
            w_router.T,
            norm_gain[None],
            final_gain[None],
            head_weights,
            w_gate[0],
            w_up[0],
            w_down[0],
            vocab_proj,
        )
        return losses, grads

    in_specs = (
        P("dp", None),
        P(),
        P(),
        P(),
        P("expert", None, "dp"),
        P("expert", None, "dp"),
        P("expert", "dp", None),
        P(),
        P(None, "dp", "expert"),
        P("dp", "expert"),
    )
    out_specs = (P(), P(None, "dp", "expert"))
    return jax.shard_map(shards, mesh=mesh, in_specs=in_specs, out_specs=out_specs, check_vma=False)
```

time: 823 us -> 204 us (0.25)
  waiting for transfers between devices: 482 us -> 0 us
  blocking collectives: 229 us -> 0 us
  Pallas kernels: 0 us -> 199 us
  starting transfers between devices: 36.6 us -> 0 us
  matrix products: 32.4 us -> 0 us
  between operations: 15.2 us -> 0.66 us
  other arithmetic: 13.4 us -> 0 us
    psum x2 -> x0, waiting for transfers between devices: 240 us -> none  [the longest x1 124 us: shards(): mixture = lax.psum(term.astype(jnp.bfloat16), 'expert').astype(jnp.float32)]
    all_gather x4 -> x0, waiting for transfers between devices: 236 us -> none  [the longest x1 93.7 us: shards(): lax.all_gather(head_weights, 'dp', axis=1, tiled=True)]
    pallas_call x0 -> x1, Pallas kernels: none -> 199 us  [shards(): pl.pallas_call(kernel, out_shape=(jax.ShapeDtypeStruct((NX,), F32), jax.S...]
    psum x2 -> x0, blocking collectives: 124 us -> none  [the longest x1 100 us: shards(): lax.psum(jnp.sum(row_weight * divergence, axis=-1), ('expert', 'dp'))]
    unnamed x1 -> x0, blocking collectives: 75.3 us -> none
    dot_general x11 -> x0, matrix products: 32.4 us -> none  [the longest x1 5.73 us: shards(): jnp.einsum('htv,dv->htd', slopes, vocab_all, preferred_element_type=jnp.f...]
    all_gather x1 -> x0, blocking collectives: 29.8 us -> none  [shards(): student_in = lax.all_gather(shares, 'expert', axis=2, tiled=True)]
    unnamed x8 -> x0, starting transfers between devices: 25.1 us -> none
  transfers between devices with their start and end apart: 16 -> 0, of which waited for: 7 -> 0; matrix products, arithmetic and copies ran while one was open for 2% -> 0% of each run, Pallas kernels for 0% -> 0%
where the time goes in v1:
time: 204 us
  Pallas kernels  199 us (98%)
  local copies, waits for them, and re-layouts  4.5 us (2%)
    pallas_call x1, Pallas kernels, shards(): pl.pallas_call(kernel, out_shape=(jax.ShapeDtypeStruct((NX,), F32), jax.S...  199 us
    unnamed x7, local copies, waits for them, and re-layouts  4.5 us

profile of v1, /device:TPU:1, one launch (start us, length us, event | category | flops | bytes accessed | tf_op | source)
XLA Modules:
  0.0 203.9 jit_solution(4888855658553343243)
XLA Ops:
  0.6 0.0 copy-start
  0.6 0.7 copy-done
  1.3 0.9 copy.12.refs_1_
  2.3 198.7 %step.1 = (f32[4]{0:T(128)}, f32[4,96,192]{2,1,0:T(8,128)}) custom-call(bf16[24,3072]{1,0:T(8,128)(2,1)} %refs_0_.1, s32[768,2]{1,0:T(8,128)} %copy.12.refs_1_, bf16[8,3072]{1,0:T(8,128)(2,1)} %bitcast.9, f32[1,3072]{1,0:T(1,128)} %bitcast.10, f32[1,3072]{1,0:T(1,128)} %bitcast.11, bf16[4,96,192]{2,1,0:T(8,128)(2,1)} %refs_5_.1, bf16[3072,128]{1,0:T(8,128)(2,1)} %bitcast.6, ...), custom_call_target="tpu_custom_call" | custom-call | tf_op jit(solution)/shard_map/step/pallas_call | solution.py:505
  201.0 0.0 copy-start.1
  201.0 0.6 copy-done.1
  201.6 0.5 copy.15
  202.1 1.8 copy.16
Async XLA Ops:
  0.6 0.7 copy-start
  201.0 0.6 copy-start.1

commit v2 on v1

v2 whole, which is shorter than its diff:
```python
import jax
import jax.numpy as jnp
from jax import lax
from jax.experimental import pallas as pl
from jax.experimental.pallas import tpu as pltpu
from jax.sharding import PartitionSpec as P

MESH = pl.DeviceIdType.MESH
F32, BF16 = jnp.float32, jnp.bfloat16
HIGHEST = lax.Precision.HIGHEST
EPS = 1e-05
NX = 4
TOK, CAP, SLOT = 24, 12, 16
N_COPIES = 480
ROWS = 48
ALL = slice(None)
NEAR, FAR = slice(0, 16), slice(16, 48)


def dot(a, b, dims=((1,), (0,)), precision=None):
    return lax.dot_general(a, b, (dims, ((), ())), precision=precision, preferred_element_type=F32)


def iota(shape, axis):
    return lax.broadcasted_iota(jnp.int32, shape, axis)


def pump(*tasks):
    live = list(tasks)
    while live:
        live = [task for task in live if next(task, live) is not live]


def body(
    nz, ny, tok_ref, routes_ref, wr_ref, ng_ref, fg_ref, hw_ref, wg_hbm, wu_hbm, wd_hbm, voc_hbm, loss_ref, out_ref,
    w_gu, wd, vg, hx, hl, hg, tk, tokf, nbs, ag, yg, uq, f96, fw, fn, gfac, sg,
    ls, tl, sums, lsum, sl, gg, osd, ord_, lhs_t, s1, s2, r1, r2, q1, q2, q3, dset, hset,
    ss, rs, lsem,
):
    dp, ex = lax.axis_index("dp"), lax.axis_index("expert")
    z, x = lax.div(dp, NX), lax.rem(dp, NX)
    y, c = lax.div(ex, 2), lax.rem(ex, 2)
    oc = 1 - c
    d_model = tok_ref.shape[1]
    half = d_model // 2
    vcols = vg.shape[2]
    kcols = d_model // ny
    grp = NX * TOK
    n_exp = wr_ref.shape[0]

    def dev(z_=None, x_=None, y_=None, c_=None):
        z_, x_ = (z if z_ is None else z_), (x if x_ is None else x_)
        y_, c_ = (y if y_ is None else y_), (c if c_ is None else c_)
        return {"dp": z_ * NX + x_, "expert": y_ * 2 + c_}

    def xo(d):
        return lax.rem(x + (d + NX), NX)

    def zo(d):
        return lax.rem(z + (d + nz), nz)

    def yo(d):
        return lax.rem(y + (d + ny), ny)

    partner = dev(c_=oc)
    over_x = [dev(x_=xo(d)) for d in range(1, NX)]
    sign = 1 - 2 * c
    z_ring = (nz, zo, lambda d: dev(z_=zo(d)))
    y_ring = (ny, yo, lambda d: dev(y_=yo(d)))
    sent = []

    def copy(src, dst, device):
        i = len(sent)
        cp = pltpu.make_async_remote_copy(
            src_ref=src, dst_ref=dst, send_sem=ss.at[i], recv_sem=rs.at[i], device_id=device, device_id_type=MESH
        )
        cp.start()
        sent.append(cp)
        return cp

    def same(ref, device):
        return copy(ref, ref, device)

    locals_ = []

    def local(src, dst):
        cp = pltpu.make_async_copy(src, dst, lsem.at[len(locals_)])
        cp.start()
        locals_.append(cp)
        return cp

    def arrive(copies):
        for cp in copies:
            cp.wait_recv()

    vrow = d_model // (nz * NX)
    quarter = lambda x_: pl.ds(pl.multiple_of(x_ * vcols, 128), vcols)
    hcols = lambda c_: pl.ds(pl.multiple_of(c_ * half, 128), half)
    ycols = lambda y_: pl.ds(pl.multiple_of(y_ * kcols, 128), kcols)
    vslot = lambda x_: pl.ds(pl.multiple_of(x_ * vrow, 16), vrow)
    in_w = [
        local(wg_hbm, w_gu.at[:, 0:128]),
        local(wu_hbm, w_gu.at[:, 128:256]),
        local(wd_hbm.at[:, hcols(c)], wd.at[0]),
        local(wd_hbm.at[:, hcols(oc)], wd.at[1]),
    ]
    in_v = local(voc_hbm.at[:, quarter(x)], vg.at[z, vslot(x), :])

    barrier = pltpu.get_barrier_semaphore()
    line_z = [dev(z_=zo(d)) for d in range(1, nz)]
    line_y = [dev(y_=yo(d)) for d in range(1, ny)]
    near = [(xo(d), c_) for d in range(1, NX) for c_ in (c, oc)] + [(x, oc)]
    plane = [dev(x_=a, c_=b) for a, b in near]
    peers = line_z + line_y + plane
    for peer in peers:
        pl.semaphore_signal(barrier, inc=1, device_id=peer, device_id_type=MESH)
    tk[c, x] = tok_ref[:, hcols(c)]
    tk[oc, x] = tok_ref[:, hcols(oc)]
    pl.semaphore_wait(barrier, len(peers))

    tcp = [copy(tok_ref.at[:, hcols(c)], tk.at[c, x], peer) for peer in over_x]

    def ring_gather(at, ring, on_arrival):
        n, off, to = ring
        h = n // 2
        a, b = same(at(off(0)), to(1)), same(at(off(0)), to(-1))
        for s in range(1, h + 1):
            yield
            a.wait_recv()
            if s < h:
                a = same(at(off(-s)), to(1))
            on_arrival(off(-s))
            if s < h:
                b.wait_recv()
                if s < h - 1:
                    b = same(at(off(s)), to(-1))
                on_arrival(off(s))

    def two_step_gather(at, ring, on_arrival):
        _, off, to = ring
        cps = {o: same(at(off(0)), to(o)) for o in (2, -2, 1, -1)}
        yield
        cps[2].wait_recv()
        cps[3] = same(at(off(-2)), to(1))
        cps[-2].wait_recv()
        cps[-3] = same(at(off(2)), to(-1))
        cps[4] = same(at(off(-2 * sign)), to(2 * sign))
        for o in (2, -2):
            on_arrival(off(-o))
        for o in (1, -1):
            cps[o].wait_recv()
            on_arrival(off(-o))
        yield
        for o in (3, -3, 4):
            cps[o].wait_recv()
            on_arrival(off(-o))

    def gather(at, ring, on_arrival=None, hooks=(), skip_x=False):
        _, off, to = ring
        take = on_arrival or (lambda ref: None)
        hooks = list(hooks)

        def hook():
            if hooks:
                hooks.pop(0)()

        on_x = []

        def over(o):
            ref = at(off(o), x, FAR)
            on_x.append((off(o), [same(ref, peer) for peer in over_x]))
            take(ref)

        bundle = lambda i: at(i, ALL, NEAR)
        near = two_step_gather(bundle, ring, lambda i: take(bundle(i)))
        cps = {o: same(at(off(0), x, FAR), to(o)) for o in (1, -1, 2, -2, 3, -3, 4)}
        if skip_x:
            take(bundle(off(0)))
            step(near)
        else:
            x_cps = [same(at(off(0), x, NEAR), peer) for peer in over_x]
        over(0)
        hook()
        for o, cp in cps.items():
            cp.wait_recv()
            over(-o)
            if o == -1 and not skip_x:
                arrive(x_cps)
                take(bundle(off(0)))
                step(near)
        hook()
        step(near)
        hook()
        for i, by_peer in on_x:
            for d, cp in zip(range(1, NX), by_peer):
                cp.wait_recv()
                take(at(i, xo(NX - d), FAR))
        hook()
        step(near)
        while hooks:
            hook()

    def scatter(fill, ring, bufs, hooks=()):
        po, ps, pr, x1s, x1r, zs, zr = bufs
        n, off, to = ring
        order = (4, 3, -3, 2, -2, 1, -1, 0)
        hooks = list(hooks)

        def hook():
            if hooks:
                hooks.pop(0)()

        fill(ps, oc)
        got = {o: copy(ps.at[off(o)], pr.at[off(o)], partner) for o in order}
        fill(po, c)
        cps = {}
        way = {o: (1, -1)[k % 2] for k, o in enumerate(order)}

        def own(o, j):
            return po[off(o), j] + pr[off(o), j].astype(F32)

        def send(i, o, value, d):
            x1s[i, off(o)] = value.astype(BF16)
            cps[i, o] = copy(x1s.at[i, off(o)], x1r.at[i, off(o)], dev(x_=xo(d)))

        def out(o):
            got[o].wait_recv()
            send(0, o, own(o, xo(2)), way[o])
            send(1, o, own(o, xo(-way[o])), -way[o])

        def middle(o):
            cps[0, o].wait_recv()
            send(2, o, own(o, xo(way[o])) + x1r[0, off(o)].astype(F32), way[o])

        def term(o):
            value = own(o, x)
            for i in (1, 2):
                cps[i, o].wait_recv()
                value = value + x1r[i, off(o)].astype(F32)
            return value

        last = []

        def along(o):
            zs[o % n] = term(o).astype(BF16)
            last.append(copy(zs.at[o % n], zr.at[o % n], to(o)))

        for o in order[:4]:
            out(o)
        hook()
        for o, later in zip(order[:4], order[4:]):
            out(later)
            middle(o)
        hook()
        for o, later in zip(order[:4], order[4:]):
            along(o)
            middle(later)
        for o in order[4:-1]:
            along(o)
        value = term(0)
        hook()
        arrive(last)
        for o in order[:-1]:
            value = value + zr[o % n].astype(F32)
        while hooks:
            hook()
        return value

    nothing = lambda *_: None

    hrows = lambda c_: pl.ds(pl.multiple_of(c_ * ROWS, 16), ROWS)
    vx = [copy(voc_hbm.at[:, quarter(xo(d))], vg.at[z, vslot(x), :], peer) for d, peer in zip(range(1, NX), over_x)]
    ex_h = copy(hw_ref.at[:, hrows(oc), :], hx, partner)

    def heads():
        ex_h.wait_recv()
        for k in range(NX):
            mine, theirs = hw_ref[k, hrows(c), :], hx[k]
            left = jnp.where(c == 0, mine, theirs)
            right = jnp.where(c == 0, theirs, mine)
            hl[k] = jnp.concatenate([left, right], axis=1)
        cps = [copy(hl.at[xo(d)], hg.at[z, x, c], peer) for d, peer in zip(range(1, NX), over_x)]
        hg[z, x, c] = hl[x]
        yield
        arrive(cps)
        forwards = []

        def forward(i):
            forwards.append(same(hg.at[i, :, c], partner))

        forward(z)
        yield from ring_gather(lambda i: hg.at[i, :, c], z_ring, forward)
        yield
        arrive(forwards)

    def vocabulary():
        arrive(vx)
        in_v.wait()
        yield from ring_gather(lambda i: vg.at[i], z_ring, nothing)

    heads, vocabulary = heads(), vocabulary()
    step = lambda task: next(task, None)

    fwd = []
    for d, cp in zip(range(1, NX), tcp):
        cp.wait_recv()
        src = xo(NX - d)
        fwd.append(same(tk.at[c, src], partner))
    pick_rows = (iota((grp, nz * grp), 1) == iota((grp, nz * grp), 0) + z * grp).astype(BF16)
    own_routes = dot(pick_rows, routes_ref[...].astype(F32).astype(BF16), ((1,), (1,)))
    e0, e1 = own_routes[:, 0:1], own_routes[:, 1:2]
    row_t = iota((grp, 1), 0)
    block = (row_t >= TOK).astype(jnp.int32) + (row_t >= 2 * TOK).astype(jnp.int32) + (row_t >= 3 * TOK).astype(jnp.int32)
    col_t = iota((grp, grp), 1)
    lower = jnp.logical_and(col_t < row_t, col_t >= block * TOK).astype(F32).astype(BF16)
    lane_e = iota((grp, n_exp), 1).astype(F32)
    hot0, hot1 = (e0 == lane_e).astype(F32), (e1 == lane_e).astype(F32)
    earlier = dot(lower, (hot0 + hot1).astype(BF16))
    at_block = (block * CAP).astype(F32)
    place0 = e0 * ROWS + at_block + jnp.sum(hot0 * earlier, axis=1, keepdims=True)
    place1 = e1 * ROWS + at_block + jnp.sum(hot1 * earlier, axis=1, keepdims=True)
    own_slot = (iota((grp, ROWS), 1) + y * ROWS).astype(F32)
    select = ((place0 == own_slot).astype(F32) + (place1 == own_slot).astype(F32)).astype(BF16)
    arrive(fwd)
    square = jnp.zeros((grp, 1), F32)
    for h in range(2):
        rows = tk[h].astype(F32).reshape(grp, half)
        square = square + jnp.sum(rows * rows, axis=1, keepdims=True)
        for j in range(NX):
            tokf[h * NX + j] = rows[:, j * kcols : (j + 1) * kcols]
    scale = lax.rsqrt(square * (1.0 / d_model) + EPS)
    router = jnp.zeros((grp, n_exp), F32)
    for i in range(2 * NX):
        cols = slice(i * kcols, (i + 1) * kcols)
        normed = (tokf[i] * scale * ng_ref[:, cols]).astype(BF16)
        nbs[i] = normed
        router = router + dot(normed, wr_ref[:, cols], ((1,), (1,)))
    for j in range(NX):
        ag[c, z, j, NEAR] = dot(select[:, NEAR], nbs[c * NX + j], ((0,), (0,))).astype(BF16)
    ag[c, z, x, FAR] = dot(select[:, FAR], nbs[c * NX + x], ((0,), (0,))).astype(BF16)

    fwd = []
    forward = lambda ref: fwd.append(same(ref, partner))
    more = lambda: step(heads)
    gather(lambda i, j, rows: ag.at[c, i, j, rows], z_ring, forward, [more, nothing, more, more], skip_x=True)
    first = jax.nn.sigmoid(jnp.sum(router * (hot0 - hot1), axis=1, keepdims=True))
    lane_f = iota((grp, n_exp * ROWS), 1).astype(F32)
    weigh = first * (place0 == lane_f).astype(F32) + (1.0 - first) * (place1 == lane_f).astype(F32)
    weigh_hi = weigh.astype(BF16)
    weigh_lo = (weigh - weigh_hi.astype(F32)).astype(BF16)
    arrive(fwd)
    for cp in in_w:
        cp.wait()

    n_rows = nz * ROWS
    pre = jnp.zeros((n_rows, 256), F32)
    for h in range(2):
        for j in range(NX):
            i = h * NX + j
            pre = pre + dot(ag[h, :, j].reshape(n_rows, kcols), w_gu[i * kcols : (i + 1) * kcols, :])
    hidden = (jax.nn.silu(pre[:, :128]) * pre[:, 128:]).astype(BF16)
    step(heads)

    def fill_rows(dst, core):
        w = wd.at[0 if core is c else 1]
        for j in range(NX):
            value = dot(hidden, w[:, j * kcols : (j + 1) * kcols])
            dst[:, j] = value.astype(dst.dtype).reshape(nz, ROWS, kcols)

    total = scatter(fill_rows, z_ring, dset, [more, lambda: pump(heads)])
    step(vocabulary)

    yg[y] = total.astype(BF16)
    across = two_step_gather(lambda i: yg.at[i], y_ring, lambda i: None)
    pump(across)
    step(vocabulary)
    outs = yg[...].reshape(n_exp * ROWS, kcols)
    mixed = tokf[c * NX + x] + dot(weigh_hi, outs) + dot(weigh_lo, outs)
    square = dot(jnp.ones((8, kcols), F32), mixed * mixed, ((1,), (1,)), HIGHEST)
    s1[:, 0:grp] = square[0:1, :]
    s1[:, grp:] = jnp.zeros((1, 128 - grp), F32)
    uq[c, x] = mixed.astype(BF16)
    ucp = [same(uq.at[c, x], peer) for peer in over_x]
    scp = [copy(s1, s2.at[x * 2 + c], peer) for peer in plane]
    fwd = [same(uq.at[c, x], partner)]
    step(heads)
    for d, cp in zip(range(1, NX), ucp):
        cp.wait_recv()
        fwd.append(same(uq.at[c, xo(NX - d)], partner))
    step(vocabulary)
    arrive(scp)
    square = s1[...]
    for a, b in near:
        square = square + s2[a * 2 + b]
    first_row = (iota((8, 128), 0) == 0).astype(F32)
    scale = lax.rsqrt(square * (1.0 / d_model) + EPS)
    scale = dot(jnp.broadcast_to(scale, (8, 128)), first_row, ((0,), (0,)), HIGHEST)[0:grp, 0:1]
    arrive(fwd)
    for h in range(2):
        for j in range(NX):
            i = h * NX + j
            cols = slice(i * kcols, (i + 1) * kcols)
            f96[:, cols] = (uq[h, j].astype(F32) * scale * fg_ref[:, cols]).astype(BF16)

    def window(z_):
        start = jnp.minimum(lax.div((z_ * NX + x) * vrow, 128) * 128, d_model - 256)
        return pl.ds(pl.multiple_of(start, 128), 256)

    tcp = [copy(f96.at[hrows(c), window(zo(d))], fw.at[z], peer) for d, peer in zip(range(1, nz), line_z)]
    fw[z] = f96[hrows(c), window(z)]
    ncp = copy(f96.at[0:16, :], fn, dev(z_=zo(-1)))

    pump(heads)
    preact = dot(f96[hrows(c), :], hg[...].reshape(d_model, kcols))
    sigma = jax.nn.sigmoid(preact)
    gfac[...] = sigma * (1.0 + preact * (1.0 - sigma))
    student = f96[hrows(c), ycols(y)].astype(F32) + preact * sigma
    sg[c, x, :, ycols(y)] = student.astype(BF16)

    fwd = []
    part = lambda i, j, rows: sg.at[c, j, rows, ALL if i is ALL else ycols(i)]
    gather(part, y_ring, forward_to(fwd, same, partner), [nothing, lambda: step(vocabulary)])
    pump(vocabulary)
    ncp.wait_recv()
    voc = vg[...].reshape(d_model, vcols)
    n_st = NX * grp
    ls[n_st : n_st + grp, :] = dot(f96[...], voc)
    ls[n_st + grp : n_st + grp + 16, :] = dot(fn[...], voc)
    ls[n_st + grp + 16 :, :] = jnp.zeros((16, vcols), F32)
    arrive(fwd)
    ls[0:n_st, :] = dot(sg[...].reshape(n_st, d_model), voc)

    def reduce_plane(src, first_in, second_in, result):
        cps = [copy(src, first_in.at[x * 2 + c], peer) for peer in plane]
        yield
        arrive(cps)
        row = src[...]
        for a, b in near:
            row = row + first_in[a * 2 + b]
        second_in[y] = row
        cps = [same(second_in.at[y], peer) for peer in line_y]
        yield
        arrive(cps)
        row = second_in[0]
        for i in range(1, ny):
            row = row + second_in[i]
        result.append(row)

    ones = jnp.ones((8, vcols), F32)
    sums[...] = dot(ones, jnp.exp(ls[...]), ((1,), (1,)), HIGHEST)[0:1, :]
    result = []
    pump(reduce_plane(sums, r1, r2, result))
    logs = jnp.log(result[0])
    n_all = ls.shape[0]
    column = dot(jnp.broadcast_to(logs, (8, n_all)), first_row, ((0,), (0,)), HIGHEST)[:, 0:1]
    tl[...] = ls[n_st : n_st + tl.shape[0], :] - column[n_st : n_st + tl.shape[0]]
    losses = [None] * NX
    row_id = iota((ROWS, 1), 0)
    n_tok = nz * grp
    for h in range(2):
        for k in range(NX):
            at = (h * NX + k) * ROWS
            logp = ls[at : at + ROWS, :] - column[at : at + ROWS]
            target = tl[h * ROWS + k + 1 : h * ROWS + k + 1 + ROWS, :]
            p = jnp.exp(target)
            weight = jnp.where(z * grp + h * ROWS + row_id + (k + 1) < n_tok, 1.0 / (n_tok - k - 1), 0.0)
            terms = jnp.sum(weight * (p * (target - logp)), axis=0, keepdims=True)
            losses[k] = terms if losses[k] is None else losses[k] + terms
            sl[h, k * ROWS : (k + 1) * ROWS, :] = (weight * (jnp.exp(logp) - p)).astype(BF16)
    for k in range(NX):
        lsum[:, k * 128 : (k + 1) * 128] = losses[k][:, :128] + losses[k][:, 128:]

    def fill_back(dst, core):
        for i in range(ny):
            value = dot(sl[core], vg[i], ((1,), (1,)))
            dst[i] = value.astype(dst.dtype).reshape(NX, ROWS, kcols)

    back = scatter(fill_back, y_ring, hset)
    gg[z, x] = (back * gfac[...]).astype(BF16)

    loss_rows = []

    def loss_task():
        result = []
        yield from reduce_plane(lsum, q1, q2, result)
        q3[z] = result[0]
        cps = [same(q3.at[z], peer) for peer in line_z]
        yield
        arrive(cps)
        row = q3[0]
        for i in range(1, nz):
            row = row + q3[i]
        loss_rows.append(row)

    def turn():
        arrive(tcp)
        lhs_t[...] = fw[...].reshape(nz * ROWS, 256).astype(F32).T.astype(BF16)

    task = loss_task()
    go_on = lambda: step(task)
    gather(lambda i, j, rows: gg.at[i, j, rows], z_ring, None, [lambda: (go_on(), turn()), go_on, go_on, go_on])

    cut = dp * vrow - jnp.minimum(lax.div(dp * vrow, 128) * 128, d_model - 256)
    lhs = lhs_t[pl.ds(pl.multiple_of(cut, 32), vrow), :]
    cols = kcols // 2
    for k in range(NX):
        o = dot(lhs, gg[:, k].reshape(nz * ROWS, kcols))
        low, high = o[:, :cols], o[:, cols:]
        osd[k] = jnp.where(c == 0, high, low)
        out_ref[k] = jnp.where(c == 0, low, high)
    ocp = copy(osd, ord_, partner)
    row = loss_rows[0]
    for k in range(NX):
        loss_ref[k] = jnp.sum(row[:, k * 128 : (k + 1) * 128])
    ocp.wait_recv()
    out_ref[...] = out_ref[...] + ord_[...]
    for cp in sent:
        cp.wait_send()


def forward_to(forwards, same, partner):
    return lambda ref: forwards.append(same(ref, partner))


def solution(mesh):
    nz, ny = mesh.shape["dp"] // NX, mesh.shape["expert"] // 2

    def shards(tokens, routes, w_router, norm_gain, w_gate, w_up, w_down, final_gain, head_weights, vocab_proj):
        d_model = tokens.shape[1]
        half = d_model // 2
        kcols = d_model // ny
        vcols = vocab_proj.shape[1] // NX
        grp = NX * TOK
        vm = pltpu.VMEM

        def scatter_set(n, own):
            return (
                vm((n, NX, ROWS, kcols), own),
                vm((n, NX, ROWS, kcols), BF16),
                vm((n, NX, ROWS, kcols), BF16),
                vm((NX - 1, n, ROWS, kcols), BF16),
                vm((NX - 1, n, ROWS, kcols), BF16),
                vm((n, ROWS, kcols), BF16),
                vm((n, ROWS, kcols), BF16),
            )

        flat = [
            vm((d_model, 256), BF16),
            vm((2, 128, half), BF16),
            vm((nz, d_model // nz, vcols), BF16),
            vm((NX, ROWS, kcols // 2), BF16),
            vm((NX, ROWS, kcols), BF16),
            vm((nz, NX, 2, ROWS, kcols), BF16),
            vm((2, NX, TOK, half), BF16),
            vm((2 * NX, grp, kcols), F32),
            vm((2 * NX, grp, kcols), BF16),
            vm((2, nz, NX, ROWS, kcols), BF16),
            vm((ny, ROWS, kcols), BF16),
            vm((2, NX, grp, kcols), BF16),
            vm((grp, d_model), BF16),
            vm((nz, ROWS, 256), BF16),
            vm((16, d_model), BF16),
            vm((ROWS, kcols), F32),
            vm((2, NX, ROWS, d_model), BF16),
            vm((512, vcols), F32),
            vm((grp + 16, vcols), F32),
            vm((1, 512), F32),
            vm((1, 512), F32),
            vm((2, NX * ROWS, vcols), BF16),
            vm((nz, NX, ROWS, kcols), BF16),
            vm((NX, 96, kcols // 2), F32),
            vm((NX, 96, kcols // 2), F32),
            vm((256, nz * ROWS), BF16),
            vm((1, 128), F32),
            vm((2 * NX, 1, 128), F32),
            vm((2 * NX, 1, 512), F32),
            vm((ny, 1, 512), F32),
            vm((2 * NX, 1, 512), F32),
            vm((ny, 1, 512), F32),
            vm((nz, 1, 512), F32),
        ]
        scratch = flat + [
            scatter_set(nz, F32),
            scatter_set(ny, F32),
            pltpu.SemaphoreType.DMA((N_COPIES,)),
            pltpu.SemaphoreType.DMA((N_COPIES,)),
            pltpu.SemaphoreType.DMA((8,)),
        ]

        def kernel(*refs):
            body(nz, ny, *refs)

        in_vmem = pl.BlockSpec(memory_space=pltpu.VMEM)
        in_hbm = pl.BlockSpec(memory_space=pl.ANY)
        losses, grads = pl.pallas_call(
            kernel,
            out_shape=(
                jax.ShapeDtypeStruct((NX,), F32),
                jax.ShapeDtypeStruct((NX, 96, kcols // 2), F32),
            ),
            in_specs=[in_vmem] * 6 + [in_hbm] * 4,
            out_specs=(pl.BlockSpec(memory_space=pltpu.SMEM), in_vmem),
            scratch_shapes=scratch,
            compiler_params=pltpu.CompilerParams(
                collective_id=0, has_side_effects=True, vmem_limit_bytes=60 * 2**20
            ),
            name="step",
        )(
            tokens,
            routes.T,
            w_router.T,
            norm_gain[None],
            final_gain[None],
            head_weights,
            w_gate[0],
            w_up[0],
            w_down[0],
            vocab_proj,
        )
        return losses, grads

    in_specs = (
        P("dp", None),
        P(),
        P(),
        P(),
        P("expert", None, "dp"),
        P("expert", None, "dp"),
        P("expert", "dp", None),
        P(),
        P(None, "dp", "expert"),
        P("dp", "expert"),
    )
    out_specs = (P(), P(None, "dp", "expert"))
    return jax.shard_map(shards, mesh=mesh, in_specs=in_specs, out_specs=out_specs, check_vma=False)
```

time: 204 us -> 160 us (0.78)
  Pallas kernels: 199 us -> 156 us
    pallas_call x1, Pallas kernels: 199 us -> 156 us  [shards(): pl.pallas_call(kernel, out_shape=(jax.ShapeDtypeStruct((NX,), F32), jax.S...]
    unnamed x7 -> x4, local copies, waits for them, and re-layouts: 4.5 us -> 2.95 us
where the time goes in v2:
time: 160 us
  Pallas kernels  156 us (98%)
  local copies, waits for them, and re-layouts  2.95 us (2%)
    pallas_call x1, Pallas kernels, shards(): pl.pallas_call(kernel, out_shape=(jax.ShapeDtypeStruct((NX,), F32), jax.S...  156 us

profile of v2, /device:TPU:1, one launch (start us, length us, event | category | flops | bytes accessed | tf_op | source)
XLA Modules:
  0.0 160.0 jit_solution(6175245372468969049)
XLA Ops:
  0.6 156.4 %step.1 = (f32[4]{0:T(128)}, f32[4,96,192]{2,1,0:T(8,128)}) custom-call(bf16[24,3072]{1,0:T(8,128)(2,1)} %refs_0_.1, s32[2,768]{1,0:T(2,128)} %bitcast.13, bf16[8,3072]{1,0:T(8,128)(2,1)} %bitcast.10, f32[1,3072]{1,0:T(1,128)} %bitcast.11, f32[1,3072]{1,0:T(1,128)} %bitcast.12, bf16[4,96,192]{2,1,0:T(8,128)(2,1)} %refs_5_.1, bf16[3072,128]{1,0:T(8,128)(2,1)} %bitcast.7, ...), custom_call_target="tpu_custom_call" | custom-call | tf_op jit(solution)/shard_map/step/pallas_call | solution.py:595
  157.1 0.0 copy-start
  157.1 0.7 copy-done
  157.7 0.5 copy.14
  158.3 1.8 %copy.15 = f32[4,96,192]{2,1,0:T(8,128)} copy(f32[4,96,192]{2,1,0:T(8,128)} %get-tuple-element.5) | data formatting | bytes 589824
Async XLA Ops:
  157.1 0.7 copy-start

commit v3 on v2

--- a/solution.py
+++ b/solution.py
@@ -32,8 +32,8 @@
 
 
 def body(
-    nz, ny, tok_ref, routes_ref, wr_ref, ng_ref, fg_ref, hw_ref, wg_hbm, wu_hbm, wd_hbm, voc_hbm, loss_ref, out_ref,
-    w_gu, wd, vg, hx, hl, hg, tk, tokf, nbs, ag, yg, uq, f96, fw, fn, gfac, sg,
+    nz, ny, tok_hbm, routes_hbm, wr_hbm, ng_hbm, fg_hbm, hw_hbm, wg_hbm, wu_hbm, wd_hbm, voc_hbm, loss_ref, out_ref,
+    tok_ref, routes_ref, wr_ref, ng_ref, fg_ref, hw_ref, w_gu, wd, vg, hx, hl, hg, tk, tokf, nbs, ag, yg, uq, f96, fw, fn, gfac, sg,
     ls, tl, sums, lsum, sl, gg, osd, ord_, lhs_t, s1, s2, r1, r2, q1, q2, q3, dset, hset,
     ss, rs, lsem,
 ):
@@ -98,6 +98,17 @@
     hcols = lambda c_: pl.ds(pl.multiple_of(c_ * half, 128), half)
     ycols = lambda y_: pl.ds(pl.multiple_of(y_ * kcols, 128), kcols)
     vslot = lambda x_: pl.ds(pl.multiple_of(x_ * vrow, 16), vrow)
+    in_tok = local(tok_hbm, tok_ref)
+    in_small = [
+        local(src, dst)
+        for src, dst in (
+            (routes_hbm, routes_ref),
+            (wr_hbm, wr_ref),
+            (ng_hbm, ng_ref),
+            (fg_hbm, fg_ref),
+            (hw_hbm, hw_ref),
+        )
+    ]
     in_w = [
         local(wg_hbm, w_gu.at[:, 0:128]),
         local(wu_hbm, w_gu.at[:, 128:256]),
@@ -114,6 +125,7 @@
     peers = line_z + line_y + plane
     for peer in peers:
         pl.semaphore_signal(barrier, inc=1, device_id=peer, device_id_type=MESH)
+    in_tok.wait()
     tk[c, x] = tok_ref[:, hcols(c)]
     tk[oc, x] = tok_ref[:, hcols(oc)]
     pl.semaphore_wait(barrier, len(peers))
@@ -270,7 +282,7 @@
 
     hrows = lambda c_: pl.ds(pl.multiple_of(c_ * ROWS, 16), ROWS)
     vx = [copy(voc_hbm.at[:, quarter(xo(d))], vg.at[z, vslot(x), :], peer) for d, peer in zip(range(1, NX), over_x)]
-    ex_h = copy(hw_ref.at[:, hrows(oc), :], hx, partner)
+    ex_h = copy(hw_hbm.at[:, hrows(oc), :], hx, partner)
 
     def heads():
         ex_h.wait_recv()
@@ -306,6 +318,8 @@
         cp.wait_recv()
         src = xo(NX - d)
         fwd.append(same(tk.at[c, src], partner))
+    for cp in in_small:
+        cp.wait()
     pick_rows = (iota((grp, nz * grp), 1) == iota((grp, nz * grp), 0) + z * grp).astype(BF16)
     own_routes = dot(pick_rows, routes_ref[...].astype(F32).astype(BF16), ((1,), (1,)))
     e0, e1 = own_routes[:, 0:1], own_routes[:, 1:2]
@@ -342,7 +356,7 @@
     fwd = []
     forward = lambda ref: fwd.append(same(ref, partner))
     more = lambda: step(heads)
-    gather(lambda i, j, rows: ag.at[c, i, j, rows], z_ring, forward, [more, nothing, more, more], skip_x=True)
+    gather(lambda i, j, rows: ag.at[c, i, j, rows], z_ring, forward, [more, nothing, more], skip_x=True)
     first = jax.nn.sigmoid(jnp.sum(router * (hot0 - hot1), axis=1, keepdims=True))
     lane_f = iota((grp, n_exp * ROWS), 1).astype(F32)
     weigh = first * (place0 == lane_f).astype(F32) + (1.0 - first) * (place1 == lane_f).astype(F32)
@@ -351,6 +365,7 @@
     arrive(fwd)
     for cp in in_w:
         cp.wait()
+    more()
 
     n_rows = nz * ROWS
     pre = jnp.zeros((n_rows, 256), F32)
@@ -359,7 +374,6 @@
             i = h * NX + j
             pre = pre + dot(ag[h, :, j].reshape(n_rows, kcols), w_gu[i * kcols : (i + 1) * kcols, :])
     hidden = (jax.nn.silu(pre[:, :128]) * pre[:, 128:]).astype(BF16)
-    step(heads)
 
     def fill_rows(dst, core):
         w = wd.at[0 if core is c else 1]
@@ -367,13 +381,14 @@
             value = dot(hidden, w[:, j * kcols : (j + 1) * kcols])
             dst[:, j] = value.astype(dst.dtype).reshape(nz, ROWS, kcols)
 
-    total = scatter(fill_rows, z_ring, dset, [more, lambda: pump(heads)])
-    step(vocabulary)
+    total = scatter(fill_rows, z_ring, dset, [more, more, lambda: (more(), step(vocabulary))])
 
     yg[y] = total.astype(BF16)
     across = two_step_gather(lambda i: yg.at[i], y_ring, lambda i: None)
+    step(across)
+    step(across)
+    step(vocabulary)
     pump(across)
-    step(vocabulary)
     outs = yg[...].reshape(n_exp * ROWS, kcols)
     mixed = tokf[c * NX + x] + dot(weigh_hi, outs) + dot(weigh_lo, outs)
     square = dot(jnp.ones((8, kcols), F32), mixed * mixed, ((1,), (1,)), HIGHEST)
@@ -475,9 +490,6 @@
             value = dot(sl[core], vg[i], ((1,), (1,)))
             dst[i] = value.astype(dst.dtype).reshape(NX, ROWS, kcols)
 
-    back = scatter(fill_back, y_ring, hset)
-    gg[z, x] = (back * gfac[...]).astype(BF16)
-
     loss_rows = []
 
     def loss_task():
@@ -498,7 +510,11 @@
 
     task = loss_task()
     go_on = lambda: step(task)
-    gather(lambda i, j, rows: gg.at[i, j, rows], z_ring, None, [lambda: (go_on(), turn()), go_on, go_on, go_on])
+    go_on()
+    back = scatter(fill_back, y_ring, hset, [go_on, go_on])
+    gg[z, x] = (back * gfac[...]).astype(BF16)
+
+    gather(lambda i, j, rows: gg.at[i, j, rows], z_ring, None, [lambda: (turn(), go_on())])
 
     cut = dp * vrow - jnp.minimum(lax.div(dp * vrow, 128) * 128, d_model - 256)
     lhs = lhs_t[pl.ds(pl.multiple_of(cut, 32), vrow), :]
@@ -545,6 +561,12 @@
             )
 
         flat = [
+            vm(tokens.shape, BF16),
+            vm(routes.shape[::-1], jnp.int32),
+            vm(w_router.shape[::-1], BF16),
+            vm((1, d_model), F32),
+            vm((1, d_model), F32),
+            vm(head_weights.shape, BF16),
             vm((d_model, 256), BF16),
             vm((2, 128, half), BF16),
             vm((nz, d_model // nz, vcols), BF16),
@@ -584,7 +606,7 @@
             scatter_set(ny, F32),
             pltpu.SemaphoreType.DMA((N_COPIES,)),
             pltpu.SemaphoreType.DMA((N_COPIES,)),
-            pltpu.SemaphoreType.DMA((8,)),
+            pltpu.SemaphoreType.DMA((16,)),
         ]
 
         def kernel(*refs):
@@ -598,7 +620,7 @@
                 jax.ShapeDtypeStruct((NX,), F32),
                 jax.ShapeDtypeStruct((NX, 96, kcols // 2), F32),
             ),
-            in_specs=[in_vmem] * 6 + [in_hbm] * 4,
+            in_specs=[in_hbm] * 10,
             out_specs=(pl.BlockSpec(memory_space=pltpu.SMEM), in_vmem),
             scratch_shapes=scratch,
             compiler_params=pltpu.CompilerParams(

time: 160 us -> 153 us (0.956)
  Pallas kernels: 156 us -> 149 us
    pallas_call x1, Pallas kernels: 156 us -> 149 us  [shards(): pl.pallas_call(kernel, out_shape=(jax.ShapeDtypeStruct((NX,), F32), jax.S...]
where the time goes in v3:
time: 153 us
  Pallas kernels  149 us (97%)
  local copies, waits for them, and re-layouts  2.95 us (2%)
    pallas_call x1, Pallas kernels, shards(): pl.pallas_call(kernel, out_shape=(jax.ShapeDtypeStruct((NX,), F32), jax.S...  149 us

profile of v3, /device:TPU:1, one launch (start us, length us, event | category | flops | bytes accessed | tf_op | source)
XLA Modules:
  0.0 153.0 jit_solution(4245436625987706778)
XLA Ops:
  0.6 149.4 %step.1 = (f32[4]{0:T(128)}, f32[4,96,192]{2,1,0:T(8,128)}) custom-call(bf16[24,3072]{1,0:T(8,128)(2,1)} %refs_0_.1, s32[2,768]{1,0:T(2,128)} %bitcast.13, bf16[8,3072]{1,0:T(8,128)(2,1)} %bitcast.10, f32[1,3072]{1,0:T(1,128)} %bitcast.11, f32[1,3072]{1,0:T(1,128)} %bitcast.12, bf16[4,96,192]{2,1,0:T(8,128)(2,1)} %refs_5_.1, bf16[3072,128]{1,0:T(8,128)(2,1)} %bitcast.7, ...), custom_call_target="tpu_custom_call" | custom-call | tf_op jit(solution)/shard_map/step/pallas_call | solution.py:617
  150.0 0.0 copy-start
  150.1 0.7 copy-done
  150.7 0.5 copy.14
  151.2 1.8 %copy.15 = f32[4,96,192]{2,1,0:T(8,128)} copy(f32[4,96,192]{2,1,0:T(8,128)} %get-tuple-element.5) | data formatting | bytes 589824
Async XLA Ops:
  150.0 0.7 copy-start

commit v4 on v3

--- a/solution.py
+++ b/solution.py
@@ -222,9 +222,12 @@
             if hooks:
                 hooks.pop(0)()
 
-        fill(ps, oc)
-        got = {o: copy(ps.at[off(o)], pr.at[off(o)], partner) for o in order}
-        fill(po, c)
+        got = {}
+        for o in order:
+            fill(ps, oc, o)
+            got[o] = copy(ps.at[off(o)], pr.at[off(o)], partner)
+        for o in order:
+            fill(po, c, o)
         cps = {}
         way = {o: (1, -1)[k % 2] for k, o in enumerate(order)}
 
@@ -313,11 +316,6 @@
     heads, vocabulary = heads(), vocabulary()
     step = lambda task: next(task, None)
 
-    fwd = []
-    for d, cp in zip(range(1, NX), tcp):
-        cp.wait_recv()
-        src = xo(NX - d)
-        fwd.append(same(tk.at[c, src], partner))
     for cp in in_small:
         cp.wait()
     pick_rows = (iota((grp, nz * grp), 1) == iota((grp, nz * grp), 0) + z * grp).astype(BF16)
@@ -335,6 +333,11 @@
     place1 = e1 * ROWS + at_block + jnp.sum(hot1 * earlier, axis=1, keepdims=True)
     own_slot = (iota((grp, ROWS), 1) + y * ROWS).astype(F32)
     select = ((place0 == own_slot).astype(F32) + (place1 == own_slot).astype(F32)).astype(BF16)
+    fwd = []
+    for d, cp in zip(range(1, NX), tcp):
+        cp.wait_recv()
+        src = xo(NX - d)
+        fwd.append(same(tk.at[c, src], partner))
     arrive(fwd)
     square = jnp.zeros((grp, 1), F32)
     for h in range(2):
@@ -375,20 +378,22 @@
             pre = pre + dot(ag[h, :, j].reshape(n_rows, kcols), w_gu[i * kcols : (i + 1) * kcols, :])
     hidden = (jax.nn.silu(pre[:, :128]) * pre[:, 128:]).astype(BF16)
 
-    def fill_rows(dst, core):
+    def fill_rows(dst, core, o):
+        if o != 4:
+            return
         w = wd.at[0 if core is c else 1]
         for j in range(NX):
             value = dot(hidden, w[:, j * kcols : (j + 1) * kcols])
             dst[:, j] = value.astype(dst.dtype).reshape(nz, ROWS, kcols)
 
-    total = scatter(fill_rows, z_ring, dset, [more, more, lambda: (more(), step(vocabulary))])
+    total = scatter(fill_rows, z_ring, dset, [nothing, more, lambda: step(vocabulary)])
 
     yg[y] = total.astype(BF16)
-    across = two_step_gather(lambda i: yg.at[i], y_ring, lambda i: None)
-    step(across)
-    step(across)
+    ycp = [same(yg.at[y], peer) for peer in line_y]
+    more()
+    arrive(ycp)
+    more()
     step(vocabulary)
-    pump(across)
     outs = yg[...].reshape(n_exp * ROWS, kcols)
     mixed = tokf[c * NX + x] + dot(weigh_hi, outs) + dot(weigh_lo, outs)
     square = dot(jnp.ones((8, kcols), F32), mixed * mixed, ((1,), (1,)), HIGHEST)
@@ -485,10 +490,9 @@
     for k in range(NX):
         lsum[:, k * 128 : (k + 1) * 128] = losses[k][:, :128] + losses[k][:, 128:]
 
-    def fill_back(dst, core):
-        for i in range(ny):
-            value = dot(sl[core], vg[i], ((1,), (1,)))
-            dst[i] = value.astype(dst.dtype).reshape(NX, ROWS, kcols)
+    def fill_back(dst, core, o):
+        value = dot(sl[core], vg[yo(o)], ((1,), (1,)))
+        dst[yo(o)] = value.astype(dst.dtype).reshape(NX, ROWS, kcols)
 
     loss_rows = []
 
@@ -522,14 +526,14 @@
     for k in range(NX):
         o = dot(lhs, gg[:, k].reshape(nz * ROWS, kcols))
         low, high = o[:, :cols], o[:, cols:]
-        osd[k] = jnp.where(c == 0, high, low)
+        osd[k] = jnp.where(c == 0, high, low).astype(BF16)
         out_ref[k] = jnp.where(c == 0, low, high)
     ocp = copy(osd, ord_, partner)
     row = loss_rows[0]
     for k in range(NX):
         loss_ref[k] = jnp.sum(row[:, k * 128 : (k + 1) * 128])
     ocp.wait_recv()
-    out_ref[...] = out_ref[...] + ord_[...]
+    out_ref[...] = out_ref[...] + ord_[...].astype(F32)
     for cp in sent:
         cp.wait_send()
 
@@ -590,8 +594,8 @@
             vm((1, 512), F32),
             vm((2, NX * ROWS, vcols), BF16),
             vm((nz, NX, ROWS, kcols), BF16),
-            vm((NX, 96, kcols // 2), F32),
-            vm((NX, 96, kcols // 2), F32),
+            vm((NX, 96, kcols // 2), BF16),
+            vm((NX, 96, kcols // 2), BF16),
             vm((256, nz * ROWS), BF16),
             vm((1, 128), F32),
             vm((2 * NX, 1, 128), F32),

time: 153 us -> 151 us (0.987)
  Pallas kernels: 149 us -> 147 us
    pallas_call x1, Pallas kernels: 149 us -> 147 us  [shards(): pl.pallas_call(kernel, out_shape=(jax.ShapeDtypeStruct((NX,), F32), jax.S...]
where the time goes in v4:
time: 151 us
  Pallas kernels  147 us (97%)
  local copies, waits for them, and re-layouts  2.95 us (2%)
    pallas_call x1, Pallas kernels, shards(): pl.pallas_call(kernel, out_shape=(jax.ShapeDtypeStruct((NX,), F32), jax.S...  147 us

profile of v4, /device:TPU:1, one launch (start us, length us, event | category | flops | bytes accessed | tf_op | source)
XLA Modules:
  0.0 150.6 jit_solution(6865076743521307057)
XLA Ops:
  0.6 147.0 %step.1 = (f32[4]{0:T(128)}, f32[4,96,192]{2,1,0:T(8,128)}) custom-call(bf16[24,3072]{1,0:T(8,128)(2,1)} %refs_0_.1, s32[2,768]{1,0:T(2,128)} %bitcast.13, bf16[8,3072]{1,0:T(8,128)(2,1)} %bitcast.10, f32[1,3072]{1,0:T(1,128)} %bitcast.11, f32[1,3072]{1,0:T(1,128)} %bitcast.12, bf16[4,96,192]{2,1,0:T(8,128)(2,1)} %refs_5_.1, bf16[3072,128]{1,0:T(8,128)(2,1)} %bitcast.7, ...), custom_call_target="tpu_custom_call" | custom-call | tf_op jit(solution)/shard_map/step/pallas_call | solution.py:621
  147.6 0.0 copy-start
  147.6 0.7 copy-done
  148.3 0.5 copy.14
  148.8 1.8 %copy.15 = f32[4,96,192]{2,1,0:T(8,128)} copy(f32[4,96,192]{2,1,0:T(8,128)} %get-tuple-element.5) | data formatting | bytes 589824
Async XLA Ops:
  147.6 0.7 copy-start

commit v5 on v4

--- a/solution.py
+++ b/solution.py
@@ -407,7 +407,6 @@
     for d, cp in zip(range(1, NX), ucp):
         cp.wait_recv()
         fwd.append(same(uq.at[c, xo(NX - d)], partner))
-    step(vocabulary)
     arrive(scp)
     square = s1[...]
     for a, b in near:
@@ -429,6 +428,7 @@
     tcp = [copy(f96.at[hrows(c), window(zo(d))], fw.at[z], peer) for d, peer in zip(range(1, nz), line_z)]
     fw[z] = f96[hrows(c), window(z)]
     ncp = copy(f96.at[0:16, :], fn, dev(z_=zo(-1)))
+    step(vocabulary)
 
     pump(heads)
     preact = dot(f96[hrows(c), :], hg[...].reshape(d_model, kcols))

time: 151 us -> 155 us (1.026)
  Pallas kernels: 147 us -> 151 us
    pallas_call x1, Pallas kernels: 147 us -> 151 us  [shards(): pl.pallas_call(kernel, out_shape=(jax.ShapeDtypeStruct((NX,), F32), jax.S...]
where the time goes in v5:
time: 155 us; the launch traced here: 154 us
  Pallas kernels  151 us (97%)
  local copies, waits for them, and re-layouts  2.95 us (2%)
    pallas_call x1, Pallas kernels, shards(): pl.pallas_call(kernel, out_shape=(jax.ShapeDtypeStruct((NX,), F32), jax.S...  151 us

profile of v5, /device:TPU:1, one launch (start us, length us, event | category | flops | bytes accessed | tf_op | source)
XLA Modules:
  0.0 154.4 jit_solution(6266315466133934899)
XLA Ops:
  0.6 150.8 %step.1 = (f32[4]{0:T(128)}, f32[4,96,192]{2,1,0:T(8,128)}) custom-call(bf16[24,3072]{1,0:T(8,128)(2,1)} %refs_0_.1, s32[2,768]{1,0:T(2,128)} %bitcast.13, bf16[8,3072]{1,0:T(8,128)(2,1)} %bitcast.10, f32[1,3072]{1,0:T(1,128)} %bitcast.11, f32[1,3072]{1,0:T(1,128)} %bitcast.12, bf16[4,96,192]{2,1,0:T(8,128)(2,1)} %refs_5_.1, bf16[3072,128]{1,0:T(8,128)(2,1)} %bitcast.7, ...), custom_call_target="tpu_custom_call" | custom-call | tf_op jit(solution)/shard_map/step/pallas_call | solution.py:621
  151.4 0.0 copy-start
  151.4 0.7 copy-done
  152.1 0.5 copy.14
  152.6 1.8 %copy.15 = f32[4,96,192]{2,1,0:T(8,128)} copy(f32[4,96,192]{2,1,0:T(8,128)} %get-tuple-element.5) | data formatting | bytes 589824
Async XLA Ops:
  151.4 0.7 copy-start
